TPU v7x, 32 devices: a whole 2x2x4 slice. The times are simulated.
32 devices in a mesh: depth: 16 (over z, y, x), samp: 2 (over core).
Axes of the slice: x: 2, y: 2, z: 4, core: 2. Of those that a mesh axis runs over, the one named last changes fastest.
Arguments:
- activations: bfloat16 [2, 16, 64, 16, 128], P('samp', 'depth'), may hold values from -6 to 6
- preact: bfloat16 [2, 16, 64, 16, 128], P('samp', 'depth'), may hold values from -6 to 6
- out_grad: bfloat16 [2, 16, 64, 16, 128], P('samp', 'depth'), may hold values from -6 to 6
- weights: bfloat16 [3, 3, 3, 128, 128], replicated, may hold values from -0.109375 to 0.109375
- master: float32 [442368], P(('depth', 'samp')), may hold values from -0.109375 to 0.109375
- moment: float32 [442368], P(('depth', 'samp')), may hold values from -4 to 4
- second: float32 [442368], P(('depth', 'samp')), may hold values from 0.1 to 1
Outputs:
- grad_input: bfloat16 [2, 16, 64, 16, 128], P('samp', 'depth')
- filter_grad: float32 [442368], P(('depth', 'samp'))
- new_moment: float32 [442368], P(('depth', 'samp'))
- new_second: float32 [442368], P(('depth', 'samp'))
- new_master: float32 [442368], P(('depth', 'samp'))
- new_weights: bfloat16 [3, 3, 3, 128, 128], replicated
All inputs are finite; a program needn't handle non-finite values.
Results may differ from a plain program's by a relative error of at most 0.001.
Values may be sent and summed in bfloat16 or wider, within the bound.
No kernel may reach another device: no remote copies, remote signals or barrier semaphores. Data moves between devices by JAX's collectives and lax.ppermute only.
A program may use at most 64 MiB of HBM per device.

v0:
```python
import functools
import math
import jax
import jax.numpy as jnp
from jax import lax
from jax.experimental import pallas as pl
from jax.experimental.pallas import tpu as pltpu
from jax.sharding import PartitionSpec as P

first_fix = 1.0
second_fix = 0.63230457524
AXES = ("depth", "samp")
ORDERS = {
    "first": ((2, 1, 3), (2, 1, 3)),
    "second": ((3, 2, 1), (3, 1, 2)),
    "line": ((3, 2, 1), (3, 2, 1)),
    "plane": ((3, 2, 1), (3, 2, 1)),
}
VMEM = pl.BlockSpec(memory_space=pltpu.VMEM)
SMEM = pl.BlockSpec(memory_space=pltpu.SMEM)
HBM = pl.BlockSpec(memory_space=pltpu.HBM)


def masks_of(stage, n):
    plain = (tuple(range(n - 1, 0, -1)),) * 2
    orders = ORDERS[stage] if n == 4 else plain
    return ((0, 0), *list(zip(*orders))[::-1])


def exchange(stage, n, terms, scales):
    got = [terms[0]]
    for t, masks in enumerate(masks_of(stage, n)):
        if t > 0:
            got.append(swap(terms[t], *(m * scale for m, scale in zip(masks, scales))))
    return got


def call(body, outs, n_in, flops=0, moved=0, scratch=(), limit=2 << 20, scalars=1):
    return pl.pallas_call(
        body,
        out_shape=outs,
        in_specs=[SMEM] * scalars + [VMEM] * n_in,
        out_specs=jax.tree.map(lambda _: VMEM, outs),
        scratch_shapes=list(scratch),
        cost_estimate=pl.CostEstimate(flops=flops, bytes_accessed=moved, transcendentals=0),
        compiler_params=pltpu.CompilerParams(vmem_limit_bytes=limit),
    )


def fill_shifted(shifted, slot, halves, width):
    plane = jnp.concatenate([half[...] for half in halves], axis=0)
    rows, chans = plane.shape
    wide = plane.astype(jnp.float32)
    column = lax.broadcasted_iota(jnp.int32, (rows, chans), 0) % width
    nxt = jnp.where(column == width - 1, 0.0, pltpu.roll(wide, rows - 1, 0))
    prv = jnp.where(column == 0, 0.0, pltpu.roll(wide, 1, 0))
    edge = jnp.zeros((width, 3 * chans), plane.dtype)
    shifted[slot, 0:width, :] = edge
    shifted[slot, width + rows : 2 * width + rows, :] = edge
    body = slice(width, width + rows)
    shifted[slot, body, 0:chans] = nxt.astype(plane.dtype)
    shifted[slot, body, chans : 2 * chans] = plane
    shifted[slot, body, 2 * chans :] = prv.astype(plane.dtype)


def planes_of(odd, refs):
    yield 0, 1, refs[0:2]
    yield 1, 2 * odd, refs[2:4]
    yield 2, 2 - 2 * odd, refs[4:6]


def filter_taps(width, act, planes, grads, shifted):
    left = act[...]
    rows, chans = left.shape
    for slot, deep, plane in planes:
        fill_shifted(shifted, slot, plane, width)
        for b in range(3):
            part = shifted[slot, (2 - b) * width : (2 - b) * width + rows, :]
            out = lax.dot_general(
                left, part, (((0,), (0,)), ((), ())), preferred_element_type=jnp.float32
            )
            for c in range(3):
                at = ((deep * 3 + b) * 3 + c) * chans
                if not isinstance(at, int):
                    at = pl.multiple_of(at, chans)
                grads[pl.ds(at, chans), :] = out[:, c * chans : (c + 1) * chans]


def pick(source, keep, send, core, step, starts):
    wide = keep.shape[1]
    for at, slot in starts:
        keep[slot] = source[pl.ds(pl.multiple_of(at + core * step, 8), wide), :]
        send[slot] = source[pl.ds(pl.multiple_of(at + (1 - core) * step, 8), wide), :]


def early_body(width, chip, step, core, act, top, bottom, edges, keep, send, shifted, grads):
    filter_taps(width, act, [(0, 0, (top, bottom))], grads, shifted)
    lead, count = edges.shape[0] // 2, keep.shape[0]
    pick(grads, keep, send, core[0], step, [(lead + k * chip, k) for k in range(count)])
    edges[0:lead, :] = grads[0:lead, :]
    edges[lead:, :] = grads[lead + count * chip :, :]


def outer_taps(width, chip, side, last, act, halves, grads, shifted):
    filter_taps(width, act, [(0, 0, halves)], grads, shifted)
    edge = grads.shape[0] - side * chip
    return last * edge, pl.multiple_of((1 - last) * side * chip, 8), edge


def near_body(width, chip, step, core, odd, act, top, bottom, rim, keep, send, shifted, grads):
    side = keep.shape[0]
    start, at, edge = outer_taps(width, chip, side, odd[0], act, (top, bottom), grads, shifted)
    pick(grads, keep, send, core[0], step, [(start + k * chip, k) for k in range(side)])
    rim[...] = grads[pl.ds(at, edge), :]


def late_body(width, chip, step, core, odd, act, top, bottom, edges, rim, keep, send, *scratch):
    shifted, grads, ends = scratch
    side = keep.shape[0] - 2
    last = 1 - odd[0]
    start, at, edge = outer_taps(width, chip, side, last, act, (top, bottom), grads, shifted)
    pick(grads, keep, send, core[0], step, [(start + k * chip, k) for k in range(side)])
    lead = chip - edge
    ends[edge:chip, :] = edges[0:lead, :]
    ends[chip : chip + lead, :] = edges[lead:, :]
    ends[pl.ds(pl.multiple_of(last * (chip + lead), 8), edge), :] = grads[pl.ds(at, edge), :]
    ends[pl.ds(pl.multiple_of((1 - last) * (chip + lead), 8), edge), :] = rim[...]
    pick(ends, keep, send, core[0], step, [(0, side), (chip, side + 1)])


def all_filter_body(width, odd, act, *refs):
    halves, (grads, shifted) = refs[:6], refs[6:]
    filter_taps(width, act, planes_of(odd[0], halves), grads, shifted)


def input_body(width, odd, weights, *refs):
    halves, (out, token, shifted) = refs[:6], refs[6:]
    rows, chans = out.shape
    total = jnp.zeros((rows, chans), jnp.float32)
    for slot, deep, plane in planes_of(odd[0], halves):
        fill_shifted(shifted, slot, plane, width)
        for b in range(3):
            part = shifted[slot, (2 - b) * width : (2 - b) * width + rows, :]
            taps = [weights[(deep * 3 + b) * 3 + c] for c in range(3)]
            total = total + lax.dot_general(
                part,
                jnp.concatenate(taps, axis=1),
                (((1,), (1,)), ((), ())),
                preferred_element_type=jnp.float32,
            )
    out[...] = total.astype(out.dtype)
    token[...] = jnp.zeros(token.shape, token.dtype)


def merge_body(n, stage, swapped, split, core, first, second, *refs):
    outs = refs[len(refs) - n :]
    terms = [r for r in refs[: len(refs) - n] if len(r.shape) == 3]
    flip = core[0] != swapped
    own = jnp.where(flip, second[0], first[0])
    group, other = jnp.where(flip, n, 1), jnp.where(flip, 1, n)
    for j, masks in enumerate(masks_of(stage, n)):
        at = own ^ jnp.where(core[0] == 0, *masks)
        for h in range(outs[j].shape[0]):
            piece = at * group + h * other if outs[j].shape[0] > 1 else at
            if not split:
                outs[j][h] = functools.reduce(lambda x, y: x + y, [term[piece] for term in terms])
                continue
            side, count = terms[2].shape[0], terms[4].shape[0]
            low, high = side + 1, side + 1 + count
            inner = (piece >= low) & (piece < high)
            upper = (piece > high).astype(jnp.int32)
            outer = jnp.clip(piece - upper * (high + 1), 0, side - 1)
            across = (piece == side) | (piece == high)
            near = (upper == (first[0] & 1)) & jnp.logical_not(across | inner)
            late = jnp.where(across, side + (piece == high).astype(jnp.int32), outer)
            early = jnp.clip(piece - low, 0, count - 1)
            rest = jnp.logical_not(inner | near)
            for chosen, pair, index in ((inner, 4, early), (near, 2, outer), (rest, 0, late)):

                @pl.when(chosen)
                def _(out=outs[j], pair=pair, index=index, h=h):
                    out[h] = terms[pair][index] + terms[pair + 1][index]


def adam_step(count, core, terms, master, moment, second):
    total = terms[0][0]
    for term in terms[1:]:
        total = total + term[0]
    size = master.shape[0]
    skip = total.shape[0] - size
    raw = jnp.where(core == 0, total[0:size], total[skip : skip + size])
    grad = raw * jnp.float32(1.0 / count**0.5)
    new_moment = 0.9 * moment[...] + 0.1 * grad
    new_second = 0.999 * second[...] + 0.001 * grad * grad
    new_master = master[...] - 0.01 * (new_moment / first_fix) / (
        jnp.sqrt(new_second / second_fix) + 1e-08
    )
    return grad, new_moment, new_second, new_master


def share_body(count, core, *refs):
    terms, (master, moment, second, share) = refs[:-4], refs[-4:]
    size, chans = master.shape
    new_master = adam_step(count, core[0], terms, master, moment, second)[3]
    share[0, 0:size, :] = new_master.astype(share.dtype)
    share[0, size:, :] = jnp.zeros((share.shape[1] - size, chans), share.dtype)


def adam_body(count, core, *refs):
    terms, (master, moment, second, _), outs = refs[:-9], refs[-9:-5], refs[-5:]
    for out, value in zip(outs, adam_step(count, core[0], terms, master, moment, second)):
        out[...] = value
    outs[4][...] = jnp.zeros(outs[4].shape, outs[4].dtype)


def gather_body(me, *refs):
    blocks = [r for r in refs[:-1] if len(r.shape) == 3]
    for k, ref in enumerate(blocks):
        refs[-1][k] = ref[0]


def place_body(n, size, groups, core, first, second, *refs):
    count = len(groups)
    own, peer, (out, done, sems) = refs[:count], refs[count : 2 * count], refs[-3:]
    copies = []
    for step in range(count * n):
        z, mask = step // count, groups[step % count]
        piece = (z ^ second[0]) * n + (mask ^ first[0])
        rows = pl.ds(pl.multiple_of(piece * 2 * size, 2 * size), 2 * size)
        copies.append(pltpu.make_async_copy(done.at[step], out.at[rows, :], sems.at[step]))

    def find(stage, c, mask):
        return [masks[c] for masks in masks_of(stage, n)].index(mask)

    def write(other):
        for step in range(count * n):
            z, group = divmod(step, count)
            for c in range(2):
                block = (own, peer)[c ^ other][group][find("line", c, z)]
                done[step, c * size : (c + 1) * size, :] = block[0:size]
            copies[step].start()

    for other in range(2):
        pl.when(core[0] == other)(functools.partial(write, other))
    for copy in copies:
        copy.wait()


def place(n, size, rows, groups, scalars, own, peer, earlier):
    chans = own[0].shape[2]
    steps = len(groups) * n
    return pl.pallas_call(
        functools.partial(place_body, n, size, groups),
        out_shape=jax.ShapeDtypeStruct((rows, chans), jnp.bfloat16),
        in_specs=[SMEM] * 3 + [VMEM] * (2 * len(groups)) + [HBM] * len(earlier),
        out_specs=HBM,
        scratch_shapes=[
            pltpu.VMEM((steps, 2 * size, chans), jnp.bfloat16),
            pltpu.SemaphoreType.DMA((steps,)),
        ],
        input_output_aliases={3 + 2 * len(groups): 0} if earlier else {},
        cost_estimate=pl.CostEstimate(flops=0, bytes_accessed=0, transcendentals=0),
        compiler_params=pltpu.CompilerParams(vmem_limit_bytes=2 << 20),
    )(*scalars, *own, *peer, *earlier)


def swap(array, *masks):
    peers = lax.axis_size("depth")
    pairs = [(2 * d + c, 2 * (d ^ masks[c]) + c) for d in range(peers) for c in range(2)]
    return lax.ppermute(array, AXES, pairs)


def swap_cores(array):
    return lax.ppermute(array, "samp", [(0, 1), (1, 0)])


def staged(n, act, halves, odd, weights, states, width, count):
    chans = act.shape[1]
    rows = 27 * chans
    pieces = n * n
    size = rows // (2 * pieces)
    wide = -(-size // 16) * 16
    step = 2 * size - wide
    depth = lax.axis_index("depth")
    one = lambda value: jnp.reshape(value, (1,)).astype(jnp.int32)
    core, first, second = one(lax.axis_index("samp")), one(depth % n), one(depth // n)
    f32 = lambda *shape: jax.ShapeDtypeStruct(shape, jnp.float32)
    b16 = lambda *shape: jax.ShapeDtypeStruct(shape, jnp.bfloat16)
    shift = pltpu.VMEM((1, act.shape[0] + 2 * width, 3 * chans), jnp.bfloat16)
    shifts = pltpu.VMEM((3, act.shape[0] + 2 * width, 3 * chans), jnp.bfloat16)
    flops = 2 * rows * chans * act.shape[0]
    third, chip = 9 * chans, 2 * size
    side = third // chip
    inner = pieces - 2 * side - 2
    edge = third - side * chip
    grads = pltpu.VMEM((third, chans), jnp.float32)
    filters = functools.partial(call, flops=flops // 3, limit=6 << 20)
    half = lambda count: (f32(count, wide, chans),) * 2
    edges, early, sent = filters(
        functools.partial(early_body, width, chip, step),
        (f32(2 * (chip - edge), chans), *half(inner)),
        3,
        scratch=[shift, grads],
    )(core, act, *halves[:2])
    early_come = swap_cores(sent)
    rim, near, sent = filters(
        functools.partial(near_body, width, chip, step),
        (f32(edge, chans), *half(side)),
        3,
        scratch=[shift, grads],
        scalars=2,
    )(core, odd, act, *halves[2:4])
    near_come = swap_cores(sent)
    late, sent = filters(
        functools.partial(late_body, width, chip, step),
        half(side + 2),
        5,
        scratch=[shift, grads, pltpu.VMEM((2 * chip, chans), jnp.float32)],
        scalars=2,
    )(core, odd, act, *halves[4:], edges, rim)
    late_come = swap_cores(sent)
    terms = (late, late_come, near, near_come, early, early_come)
    parts = call(
        functools.partial(merge_body, n, "first", 0, True), (f32(n, wide, chans),) * n, 6, scalars=3
    )(core, first, second, *terms)
    got = exchange("first", n, parts, (1, n))
    grad_input, token = call(
        functools.partial(input_body, width),
        (b16(*act.shape), f32(8, chans)),
        7,
        flops=flops,
        moved=4 << 20,
        scratch=[shifts],
        limit=6 << 20,
    )(odd, weights, *halves)
    parts = call(
        functools.partial(merge_body, n, "second", 1, False),
        (f32(1, wide, chans),) * n,
        n + 1,
        scalars=3,
    )(core, first, second, *got, token)
    got = exchange("second", n, parts, (n, 1))
    states = [s.reshape(size, chans) for s in states]
    share = call(functools.partial(share_body, count), b16(1, wide, chans), n + 3)(
        core, *got, *states
    )
    *fresh, token = call(
        functools.partial(adam_body, count),
        (f32(size, chans),) * 4 + (f32(8, chans),),
        n + 4,
    )(core, *got, *states, share)
    got = exchange("line", n, [share] * n, (n, n))
    line = call(gather_body, b16(n, wide, chans), n + 1)(core, *got, token)
    own = exchange("plane", n, [line] * n, (1, 1))
    peer = []
    for block in own:
        peer.append(swap_cores(block))
    new_weights, where = [], [list(zip(*masks_of("plane", n)))[c] for c in range(2)]
    assert where[0] == where[1]
    at = (core, first, second)
    for chosen in ((0, n - 1), tuple(range(1, n - 1))):
        groups = tuple(where[0][t] for t in chosen)
        mine, theirs = [own[t] for t in chosen], [peer[t] for t in chosen]
        new_weights = [place(n, size, rows, groups, at, mine, theirs, new_weights)]
    new_weights = new_weights[0]
    return grad_input, [x.reshape(-1) for x in fresh], new_weights


def plain(act, halves, odd, weights, states, width, count):
    chans = act.shape[1]
    rows = 27 * chans
    shift = pltpu.VMEM((3, act.shape[0] + 2 * width, 3 * chans), jnp.bfloat16)
    grads = call(
        functools.partial(all_filter_body, width),
        jax.ShapeDtypeStruct((rows, chans), jnp.float32),
        7,
        scratch=[shift],
        limit=6 << 20,
    )(odd, act, *halves)
    grad_input, _ = call(
        functools.partial(input_body, width),
        (
            jax.ShapeDtypeStruct(act.shape, jnp.bfloat16),
            jax.ShapeDtypeStruct((8, chans), jnp.float32),
        ),
        7,
        scratch=[shift],
        limit=6 << 20,
    )(odd, weights, *halves)
    total = lax.psum_scatter(grads.reshape(-1), AXES, scatter_dimension=0, tiled=True)
    master, moment, second = states
    grad = total * jnp.float32(1.0 / count**0.5)
    new_moment = 0.9 * moment + 0.1 * grad
    new_second = 0.999 * second + 0.001 * grad * grad
    new_master = master - 0.01 * (new_moment / first_fix) / (
        jnp.sqrt(new_second / second_fix) + 1e-08
    )
    whole = lax.all_gather(new_master.astype(jnp.bfloat16), AXES, axis=0, tiled=True)
    return grad_input, [grad, new_moment, new_second, new_master], whole


def neighbours(top, bottom):
    peers = lax.axis_size("depth")
    move = lambda array, pairs: lax.ppermute(array, "depth", pairs)
    partner = [(i, i ^ 1) for i in range(peers)]
    direct = [(i - 1, i) for i in range(2, peers, 2)] + [(i + 1, i) for i in range(1, peers - 1, 2)]
    relayed = [(i - 2, i) for i in range(2, peers, 2)] + [(i + 2, i) for i in range(1, peers - 1, 2)]
    partner_top = move(top, partner)
    partner_bottom = move(bottom, partner)
    other_bottom = move(bottom, direct)
    other_top = move(partner_top, relayed)
    return (top, bottom, partner_top, partner_bottom, other_top, other_bottom)


def local(n, activations, preact, out_grad, weights, master, moment, second):
    samples, planes, height, width, chans = activations.shape
    count = samples * lax.axis_size("samp") * planes * lax.axis_size("depth") * height * width
    act = activations.reshape(-1, chans)
    half = act.shape[0] // 2

    def cotangent(part):
        slope = jnp.where(preact.reshape(-1, chans)[part] > 0, jnp.float32(1.0), jnp.float32(0.01))
        return (out_grad.reshape(-1, chans)[part].astype(jnp.float32) * slope).astype(jnp.bfloat16)

    halves = neighbours(cotangent(slice(0, half)), cotangent(slice(half, None)))
    odd = jnp.reshape(lax.axis_index("depth") % 2, (1,)).astype(jnp.int32)
    taps = weights.reshape(27, chans, chans)
    states = (master, moment, second)
    if n:
        result = staged(n, act, halves, odd, taps, states, width, count)
    else:
        result = plain(act, halves, odd, taps, states, width, count)
    grad_input, fresh, whole = result
    return (grad_input.reshape(activations.shape), *fresh, whole.reshape(weights.shape))


def stages(mesh):
    n = math.isqrt(mesh.shape["depth"])
    ready = mesh.shape["samp"] == 2 and n * n == mesh.shape["depth"] and n & (n - 1) == 0
    return n if ready else 0


def solution(mesh):
    split = P("samp", "depth", None, None, None)
    shard = P(AXES)
    n = stages(mesh)

    def body(*args):
        return local(n, *args)

    return jax.shard_map(
        body,
        mesh=mesh,
        in_specs=(split, split, split, P(), shard, shard, shard),
        out_specs=(split, shard, shard, shard, shard, P()),
        check_vma=False,
    )
```

profile of v0, /device:TPU:0, one launch (start us, length us, event | category | flops | bytes accessed | tf_op | source)
XLA Modules:
  0.0 58.6 jit_solution(16850661578186264251)
XLA Ops:
  0.6 1.2 %multiply_convert_fusion = (bf16[1,1,32,16,128]{4,3,2,1,0:T(8,128)(2,1)S(1)}, bf16[1,1,32,16,128]{4,3,2,1,0:T(8,128)(2,1)S(1)}) fusion(bf16[1,1,64,16,128]{4,3,2,1,0:T(8,128)(2,1)} %param.8, bf16[1,1,64,16,128]{4,3,2,1,0:T(8,128)(2,1)} %param.9), kind=kLoop, calls=%fused_computation | loop fusion | flops 655360 | bytes 786432 | tf_op jit(solution)/shard_map/convert_element_type | solution.py:423
  1.9 3.0 %collective-permute-start = (bf16[512,128]{1,0:T(8,128)(2,1)S(1)}, bf16[512,128]{1,0:T(8,128)(2,1)S(1)}, u32[]{:S(2)}, u32[]{:S(2)}) collective-permute-start(bf16[512,128]{1,0:T(8,128)(2,1)S(1)} %bitcast.27), channel_id=1, source_target_pairs={{0,2},{2,0},{4,6},{6,4},{8,10},{10,8},{12,14},{14,12},{16,18},{18,... | collective-permute-start | bytes 393224 | tf_op jit(solution)/shard_map/ppermute | solution.py:404
  5.0 0.7 %collective-permute-start.3 = (bf16[512,128]{1,0:T(8,128)(2,1)S(1)}, bf16[512,128]{1,0:T(8,128)(2,1)S(1)}, u32[]{:S(2)}, u32[]{:S(2)}) collective-permute-start(bf16[512,128]{1,0:T(8,128)(2,1)S(1)} %bitcast.24), channel_id=1, source_target_pairs={{2,4},{6,8},{10,12},{14,16},{18,20},{22,24},{26,28},{4,2},{8,6},{1... | collective-permute-start | bytes 393224 | tf_op jit(solution)/shard_map/ppermute | solution.py:404
  5.7 3.6 %collective-permute-done.refs_2_.top = bf16[512,128]{1,0:T(8,128)(2,1)S(1)} collective-permute-done((bf16[512,128]{1,0:T(8,128)(2,1)S(1)}, bf16[512,128]{1,0:T(8,128)(2,1)S(1)}, u32[]{:S(2)}, u32[]{:S(2)}) %collective-permute-start) | collective-permute-done | bytes 131104 | tf_op jit(solution)/shard_map/ppermute | solution.py:404
  9.3 3.9 %collective-permute-start.2 = (bf16[512,128]{1,0:T(8,128)(2,1)S(1)}, bf16[512,128]{1,0:T(8,128)(2,1)S(1)}, u32[]{:S(2)}, u32[]{:S(2)}) collective-permute-start(bf16[512,128]{1,0:T(8,128)(2,1)S(1)} %collective-permute-done.refs_2_.top), channel_id=1, source_target_pairs={{0,4},{4,8},{8,12},{12,16},{16,20},{20,24},{24,28},{6,2},{10,6},{1... | collective-permute-start | bytes 393224 | tf_op jit(solution)/shard_map/ppermute | solution.py:404
  13.2 0.8 %shard_map.119 = (f32[288,128]{1,0:T(8,128)S(1)}, f32[4,112,128]{2,1,0:T(8,128)S(1)}, f32[4,112,128]{2,1,0:T(8,128)S(1)}) custom-call(s32[1]{0:T(128)} %bitcast.5.core.me, bf16[1024,128]{1,0:T(8,128)(2,1)S(1)} %bitcast.31, bf16[512,128]{1,0:T(8,128)(2,1)S(1)} %bitcast.28, bf16[512,128]{1,0:T(8,128)(2,1)S(1)} %bitcast.25), custom_call_target="tpu_custom_call" | custom-call | flops 301989888 | tf_op jit(solution)/shard_map/pallas_call | solution.py:299
  14.1 0.9 %shard_map.120 = (f32[72,128]{1,0:T(8,128)S(1)}, f32[5,112,128]{2,1,0:T(8,128)S(1)}, f32[5,112,128]{2,1,0:T(8,128)S(1)}) custom-call(s32[1]{0:T(128)} %bitcast.5.core.me, s32[1]{0:T(128)} %bitcast.odd, bf16[1024,128]{1,0:T(8,128)(2,1)S(1)} %bitcast.32, bf16[512,128]{1,0:T(8,128)(2,1)S(1)} %collective-permute-done.refs_2_.top, ...), custom_call_target="tpu_custom_call" | custom-call | flops 301989888 | tf_op jit(solution)/shard_map/pallas_call | solution.py:306
  15.0 0.8 %collective-permute-done.2.refs_4_.top = bf16[512,128]{1,0:T(8,128)(2,1)S(1)} collective-permute-done((bf16[512,128]{1,0:T(8,128)(2,1)S(1)}, bf16[512,128]{1,0:T(8,128)(2,1)S(1)}, u32[]{:S(2)}, u32[]{:S(2)}) %collective-permute-start.2) | collective-permute-done | bytes 131104 | tf_op jit(solution)/shard_map/ppermute | solution.py:404
  15.8 0.9 %shard_map.121 = (f32[7,112,128]{2,1,0:T(8,128)S(1)}, f32[7,112,128]{2,1,0:T(8,128)S(1)}) custom-call(s32[1]{0:T(128)} %bitcast.5.core.me, s32[1]{0:T(128)} %bitcast.odd, bf16[1024,128]{1,0:T(8,128)(2,1)S(1)} %bitcast.33, bf16[512,128]{1,0:T(8,128)(2,1)S(1)} %collective-permute-done.2.refs_4_.top, ...), custom_call_target="tpu_custom_call" | custom-call | flops 301989888 | tf_op jit(solution)/shard_map/pallas_call | solution.py:314
  17.4 1.9 %collective-permute-done.6.refs_5_ = f32[4,112,128]{2,1,0:T(8,128)S(1)} collective-permute-done((f32[4,112,128]{2,1,0:T(8,128)S(1)}, f32[4,112,128]{2,1,0:T(8,128)S(1)}, u32[]{:S(2)}, u32[]{:S(2)}) %collective-permute-start.6) | collective-permute-done | bytes 229408 | tf_op jit(solution)/shard_map/ppermute | solution.py:274
  19.7 4.2 %collective-permute-start.7 = (f32[4,112,128]{2,1,0:T(8,128)S(1)}, f32[4,112,128]{2,1,0:T(8,128)S(1)}, u32[]{:S(2)}, u32[]{:S(2)}) collective-permute-start(f32[4,112,128]{2,1,0:T(8,128)S(1)} %get-tuple-element.39), channel_id=1, source_target_pairs={{0,6},{1,25},{2,4},{3,27},{4,2},{5,29},{6,0},{7,31},{8,14},{9,17},... | collective-permute-start | bytes 688136 | tf_op jit(solution)/shard_map/ppermute | solution.py:270
  23.9 0.6 %collective-permute-start.9 = (f32[4,112,128]{2,1,0:T(8,128)S(1)}, f32[4,112,128]{2,1,0:T(8,128)S(1)}, u32[]{:S(2)}, u32[]{:S(2)}) collective-permute-start(f32[4,112,128]{2,1,0:T(8,128)S(1)} %get-tuple-element.41), channel_id=1, source_target_pairs={{0,4},{1,17},{2,6},{3,19},{4,0},{5,21},{6,2},{7,23},{8,12},{9,25},... | collective-permute-start | bytes 688136 | tf_op jit(solution)/shard_map/ppermute | solution.py:270
  24.5 3.0 %shard_map.118 = (bf16[1024,128]{1,0:T(8,128)(2,1)}, f32[8,128]{1,0:T(8,128)S(1)}) custom-call(s32[1]{0:T(128)} %bitcast.odd, bf16[27,128,128]{2,1,0:T(8,128)(2,1)S(1)} %bitcast.30, bf16[512,128]{1,0:T(8,128)(2,1)S(1)} %bitcast.29, bf16[512,128]{1,0:T(8,128)(2,1)S(1)} %bitcast.26, bf16[512,128]{1,0:T(8,128)(2,1)S(1)} %collective-permute-done.refs_2_.top, ...), custom_call_target="tpu_custom_call" | custom-call | flops 905969664 | bytes 4194304 | tf_op jit(solution)/shard_map/pallas_call | solution.py:327
  27.9 2.2 %collective-permute-done.8.refs_2_ = f32[4,112,128]{2,1,0:T(8,128)S(1)} collective-permute-done((f32[4,112,128]{2,1,0:T(8,128)S(1)}, f32[4,112,128]{2,1,0:T(8,128)S(1)}, u32[]{:S(2)}, u32[]{:S(2)}) %collective-permute-start.8) | collective-permute-done | bytes 229408 | tf_op jit(solution)/shard_map/ppermute | solution.py:270
  30.4 2.1 %collective-permute-start.10 = (f32[1,112,128]{2,1,0:T(8,128)S(1)}, f32[1,112,128]{2,1,0:T(8,128)S(1)}, u32[]{:S(2)}, u32[]{:S(2)}) collective-permute-start(f32[1,112,128]{2,1,0:T(8,128)S(1)} %get-tuple-element.44), channel_id=1, source_target_pairs={{0,8},{1,5},{2,10},{3,7},{4,12},{5,1},{6,14},{7,3},{8,0},{9,13},{1... | collective-permute-start | bytes 172040 | tf_op jit(solution)/shard_map/ppermute | solution.py:270
  32.5 2.6 %collective-permute-start.11 = (f32[1,112,128]{2,1,0:T(8,128)S(1)}, f32[1,112,128]{2,1,0:T(8,128)S(1)}, u32[]{:S(2)}, u32[]{:S(2)}) collective-permute-start(f32[1,112,128]{2,1,0:T(8,128)S(1)} %get-tuple-element.45), channel_id=1, source_target_pairs={{0,16},{1,3},{2,18},{3,1},{4,20},{5,7},{6,22},{7,5},{8,24},{9,11},... | collective-permute-start | bytes 172040 | tf_op jit(solution)/shard_map/ppermute | solution.py:270
  35.1 0.5 collective-permute-done.10.refs_1_
  35.6 2.6 %collective-permute-done.11.refs_2_ = f32[1,112,128]{2,1,0:T(8,128)S(1)} collective-permute-done((f32[1,112,128]{2,1,0:T(8,128)S(1)}, f32[1,112,128]{2,1,0:T(8,128)S(1)}, u32[]{:S(2)}, u32[]{:S(2)}) %collective-permute-start.11) | collective-permute-done | bytes 57376 | tf_op jit(solution)/shard_map/ppermute | solution.py:270
  38.2 2.9 %collective-permute-done.12.refs_3_ = f32[1,112,128]{2,1,0:T(8,128)S(1)} collective-permute-done((f32[1,112,128]{2,1,0:T(8,128)S(1)}, f32[1,112,128]{2,1,0:T(8,128)S(1)}, u32[]{:S(2)}, u32[]{:S(2)}) %collective-permute-start.12) | collective-permute-done | bytes 57376 | tf_op jit(solution)/shard_map/ppermute | solution.py:270
  41.2 0.8 %collective-permute-start.15 = (bf16[1,112,128]{2,1,0:T(8,128)(2,1)S(1)}, bf16[1,112,128]{2,1,0:T(8,128)(2,1)S(1)}, u32[]{:S(2)}, u32[]{:S(2)}) collective-permute-start(bf16[1,112,128]{2,1,0:T(8,128)(2,1)S(1)} %shard_map.124.refs_7_.refs_0_), channel_id=1, source_target_pairs={{0,24},{1,25},{2,26},{3,27},{4,28},{5,29},{6,30},{7,31},{8,16},{9,... | collective-permute-start | bytes 86024 | tf_op jit(solution)/shard_map/ppermute | solution.py:270
  42.0 3.7 %collective-permute-start.13 = (bf16[1,112,128]{2,1,0:T(8,128)(2,1)S(1)}, bf16[1,112,128]{2,1,0:T(8,128)(2,1)S(1)}, u32[]{:S(2)}, u32[]{:S(2)}) collective-permute-start(bf16[1,112,128]{2,1,0:T(8,128)(2,1)S(1)} %shard_map.124.refs_7_.refs_0_), channel_id=1, source_target_pairs={{0,8},{1,9},{2,10},{3,11},{4,12},{5,13},{6,14},{7,15},{8,0},{9,1},... | collective-permute-start | bytes 86024 | tf_op jit(solution)/shard_map/ppermute | solution.py:270
  45.6 0.7 %shard_map.125 = (f32[108,128]{1,0:T(8,128)}, f32[108,128]{1,0:T(8,128)}, f32[108,128]{1,0:T(8,128)}, f32[108,128]{1,0:T(8,128)}, f32[8,128]{1,0:T(8,128)S(1)}) custom-call(s32[1]{0:T(128)} %bitcast.5.core.me, f32[1,112,128]{2,1,0:T(8,128)S(1)} %get-tuple-element.43.refs_0_, f32[1,112,128]{2,1,0:T(8,128)S(1)} %collective-permute-done.10.refs_1_, ...), custom_call_target="tpu_custom_call" | custom-call | tf_op jit(solution)/shard_map/pallas_call | solution.py:347
  46.4 0.6 %collective-permute-done.15.refs_3_ = bf16[1,112,128]{2,1,0:T(8,128)(2,1)S(1)} collective-permute-done((bf16[1,112,128]{2,1,0:T(8,128)(2,1)S(1)}, bf16[1,112,128]{2,1,0:T(8,128)(2,1)S(1)}, u32[]{:S(2)}, u32[]{:S(2)}) %collective-permute-start.15) | collective-permute-done | bytes 28704 | tf_op jit(solution)/shard_map/ppermute | solution.py:270
  47.0 0.7 %collective-permute-done.14.refs_2_ = bf16[1,112,128]{2,1,0:T(8,128)(2,1)S(1)} collective-permute-done((bf16[1,112,128]{2,1,0:T(8,128)(2,1)S(1)}, bf16[1,112,128]{2,1,0:T(8,128)(2,1)S(1)}, u32[]{:S(2)}, u32[]{:S(2)}) %collective-permute-start.14) | collective-permute-done | bytes 28704 | tf_op jit(solution)/shard_map/ppermute | solution.py:270
  48.0 1.4 %collective-permute-start.20 = (bf16[4,112,128]{2,1,0:T(8,128)(2,1)S(1)}, bf16[4,112,128]{2,1,0:T(8,128)(2,1)S(1)}, u32[]{:S(2)}, u32[]{:S(2)}) collective-permute-start(bf16[4,112,128]{2,1,0:T(8,128)(2,1)S(1)} %shard_map.126.refs_0_), channel_id=1, source_target_pairs={{0,6},{1,7},{2,4},{3,5},{4,2},{5,3},{6,0},{7,1},{8,14},{9,15},{10,... | collective-permute-start | bytes 344072 | tf_op jit(solution)/shard_map/ppermute | solution.py:270
  49.4 1.0 %collective-permute-start.17 = (bf16[4,112,128]{2,1,0:T(8,128)(2,1)S(1)}, bf16[4,112,128]{2,1,0:T(8,128)(2,1)S(1)}, u32[]{:S(2)}, u32[]{:S(2)}) collective-permute-start(bf16[4,112,128]{2,1,0:T(8,128)(2,1)S(1)} %shard_map.126.refs_0_), channel_id=1, source_target_pairs={{0,4},{1,5},{2,6},{3,7},{4,0},{5,1},{6,2},{7,3},{8,12},{9,13},{10,... | collective-permute-start | bytes 344072 | tf_op jit(solution)/shard_map/ppermute | solution.py:270
  50.4 1.1 %collective-permute-start.16 = (bf16[4,112,128]{2,1,0:T(8,128)(2,1)S(1)}, bf16[4,112,128]{2,1,0:T(8,128)(2,1)S(1)}, u32[]{:S(2)}, u32[]{:S(2)}) collective-permute-start(bf16[4,112,128]{2,1,0:T(8,128)(2,1)S(1)} %shard_map.126.refs_0_), channel_id=1, source_target_pairs={{0,2},{1,3},{2,0},{3,1},{4,6},{5,7},{6,4},{7,5},{8,10},{9,11},{10,... | collective-permute-start | bytes 344072 | tf_op jit(solution)/shard_map/ppermute | solution.py:270
  51.6 3.4 %collective-permute-done.20.refs_1_ = bf16[4,112,128]{2,1,0:T(8,128)(2,1)S(1)} collective-permute-done((bf16[4,112,128]{2,1,0:T(8,128)(2,1)S(1)}, bf16[4,112,128]{2,1,0:T(8,128)(2,1)S(1)}, u32[]{:S(2)}, u32[]{:S(2)}) %collective-permute-start.20) | collective-permute-done | bytes 114720 | tf_op jit(solution)/shard_map/ppermute | solution.py:270
  55.0 1.3 %collective-permute-done.17.refs_1_ = bf16[4,112,128]{2,1,0:T(8,128)(2,1)S(1)} collective-permute-done((bf16[4,112,128]{2,1,0:T(8,128)(2,1)S(1)}, bf16[4,112,128]{2,1,0:T(8,128)(2,1)S(1)}, u32[]{:S(2)}, u32[]{:S(2)}) %collective-permute-start.17) | collective-permute-done | bytes 114720 | tf_op jit(solution)/shard_map/ppermute | solution.py:270
  56.3 0.5 collective-permute-start.18
  56.8 0.8 %shard_map.127.refs_4_ = bf16[3456,128]{1,0:T(8,128)(2,1)} custom-call(s32[1]{0:T(128)} %bitcast.5.core.me, s32[1]{0:T(128)} %bitcast.6.first, s32[1]{0:T(128)} %bitcast.7.second, bf16[4,112,128]{2,1,0:T(8,128)(2,1)S(1)} %shard_map.126.refs_0_, bf16[4,112,128]{2,1,0:T(8,128)(2,1)S(1)} %collective-permute-done.20.refs_1_, ...), custom_call_target="tpu_custom_call" | custom-call | tf_op jit(solution)/shard_map/pallas_call | solution.py:252
  57.8 0.8 %shard_map.128 = bf16[3456,128]{1,0:T(8,128)(2,1)} custom-call(s32[1]{0:T(128)} %bitcast.5.core.me, s32[1]{0:T(128)} %bitcast.6.first, s32[1]{0:T(128)} %bitcast.7.second, bf16[4,112,128]{2,1,0:T(8,128)(2,1)S(1)} %collective-permute-done.16.refs_0_, bf16[4,112,128]{2,1,0:T(8,128)(2,1)S(1)} %collective-permute-done.17.refs_1_, ...), custom_call_target="tpu_custom_call", output_to_operand_aliasing={{}: (7, {})} | custom-call | tf_op jit(solution)/shard_map/pallas_call | solution.py:252
  (36 shorter events, 2.4 us)
Async XLA Ops:
  0.6 12.6 %copy-start.4 = (bf16[1,1,64,16,128]{4,3,2,1,0:T(8,128)(2,1)S(1)}, bf16[1,1,64,16,128]{4,3,2,1,0:T(8,128)(2,1)}, u32[]{:S(2)}) copy-start(bf16[1,1,64,16,128]{4,3,2,1,0:T(8,128)(2,1)} %param.7) | copy-start | bytes 786436
  1.9 7.4 %collective-permute-start = (bf16[512,128]{1,0:T(8,128)(2,1)S(1)}, bf16[512,128]{1,0:T(8,128)(2,1)S(1)}, u32[]{:S(2)}, u32[]{:S(2)}) collective-permute-start(bf16[512,128]{1,0:T(8,128)(2,1)S(1)} %bitcast.27), channel_id=1, source_target_pairs={{0,2},{2,0},{4,6},{6,4},{8,10},{10,8},{12,14},{14,12},{16,18},{18,... | collective-permute-start | bytes 393224 | tf_op jit(solution)/shard_map/ppermute | solution.py:404
  4.9 9.2 %collective-permute-start.1 = (bf16[512,128]{1,0:T(8,128)(2,1)S(1)}, bf16[512,128]{1,0:T(8,128)(2,1)S(1)}, u32[]{:S(2)}, u32[]{:S(2)}) collective-permute-start(bf16[512,128]{1,0:T(8,128)(2,1)S(1)} %bitcast.23), channel_id=1, source_target_pairs={{0,2},{2,0},{4,6},{6,4},{8,10},{10,8},{12,14},{14,12},{16,18},{18,... | collective-permute-start | bytes 393224 | tf_op jit(solution)/shard_map/ppermute | solution.py:404
  5.0 10.0 %collective-permute-start.3 = (bf16[512,128]{1,0:T(8,128)(2,1)S(1)}, bf16[512,128]{1,0:T(8,128)(2,1)S(1)}, u32[]{:S(2)}, u32[]{:S(2)}) collective-permute-start(bf16[512,128]{1,0:T(8,128)(2,1)S(1)} %bitcast.24), channel_id=1, source_target_pairs={{2,4},{6,8},{10,12},{14,16},{18,20},{22,24},{26,28},{4,2},{8,6},{1... | collective-permute-start | bytes 393224 | tf_op jit(solution)/shard_map/ppermute | solution.py:404
  9.3 6.6 %collective-permute-start.2 = (bf16[512,128]{1,0:T(8,128)(2,1)S(1)}, bf16[512,128]{1,0:T(8,128)(2,1)S(1)}, u32[]{:S(2)}, u32[]{:S(2)}) collective-permute-start(bf16[512,128]{1,0:T(8,128)(2,1)S(1)} %collective-permute-done.refs_2_.top), channel_id=1, source_target_pairs={{0,4},{4,8},{8,12},{12,16},{16,20},{20,24},{24,28},{6,2},{10,6},{1... | collective-permute-start | bytes 393224 | tf_op jit(solution)/shard_map/ppermute | solution.py:404
  16.7 2.5 %collective-permute-start.4 = (f32[7,112,128]{2,1,0:T(8,128)S(1)}, f32[7,112,128]{2,1,0:T(8,128)S(1)}, u32[]{:S(2)}, u32[]{:S(2)}) collective-permute-start(f32[7,112,128]{2,1,0:T(8,128)S(1)} %get-tuple-element.33), channel_id=1, source_target_pairs={{0,1},{1,0},{2,3},{3,2},{4,5},{5,4},{6,7},{7,6},{8,9},{9,8},{10,11... | collective-permute-start | bytes 1204232 | tf_op jit(solution)/shard_map/ppermute | solution.py:274
  16.8 2.5 %collective-permute-start.5 = (f32[5,112,128]{2,1,0:T(8,128)S(1)}, f32[5,112,128]{2,1,0:T(8,128)S(1)}, u32[]{:S(2)}, u32[]{:S(2)}) collective-permute-start(f32[5,112,128]{2,1,0:T(8,128)S(1)} %get-tuple-element.35), channel_id=1, source_target_pairs={{0,1},{1,0},{2,3},{3,2},{4,5},{5,4},{6,7},{7,6},{8,9},{9,8},{10,11... | collective-permute-start | bytes 860168 | tf_op jit(solution)/shard_map/ppermute | solution.py:274
  17.3 2.0 %collective-permute-start.6 = (f32[4,112,128]{2,1,0:T(8,128)S(1)}, f32[4,112,128]{2,1,0:T(8,128)S(1)}, u32[]{:S(2)}, u32[]{:S(2)}) collective-permute-start(f32[4,112,128]{2,1,0:T(8,128)S(1)} %get-tuple-element.37), channel_id=1, source_target_pairs={{0,1},{1,0},{2,3},{3,2},{4,5},{5,4},{6,7},{7,6},{8,9},{9,8},{10,11... | collective-permute-start | bytes 688136 | tf_op jit(solution)/shard_map/ppermute | solution.py:274
  19.2 5.3 %copy-start.3 = (bf16[3,3,3,128,128]{4,3,2,1,0:T(8,128)(2,1)S(1)}, bf16[3,3,3,128,128]{4,3,2,1,0:T(8,128)(2,1)}, u32[]{:S(2)}) copy-start(bf16[3,3,3,128,128]{4,3,2,1,0:T(8,128)(2,1)} %param.10) | copy-start | bytes 2654212
  19.7 8.3 %collective-permute-start.7 = (f32[4,112,128]{2,1,0:T(8,128)S(1)}, f32[4,112,128]{2,1,0:T(8,128)S(1)}, u32[]{:S(2)}, u32[]{:S(2)}) collective-permute-start(f32[4,112,128]{2,1,0:T(8,128)S(1)} %get-tuple-element.39), channel_id=1, source_target_pairs={{0,6},{1,25},{2,4},{3,27},{4,2},{5,29},{6,0},{7,31},{8,14},{9,17},... | collective-permute-start | bytes 688136 | tf_op jit(solution)/shard_map/ppermute | solution.py:270
  23.9 6.2 %collective-permute-start.8 = (f32[4,112,128]{2,1,0:T(8,128)S(1)}, f32[4,112,128]{2,1,0:T(8,128)S(1)}, u32[]{:S(2)}, u32[]{:S(2)}) collective-permute-start(f32[4,112,128]{2,1,0:T(8,128)S(1)} %get-tuple-element.40), channel_id=1, source_target_pairs={{0,2},{1,9},{2,0},{3,11},{4,6},{5,13},{6,4},{7,15},{8,10},{9,1},{1... | collective-permute-start | bytes 688136 | tf_op jit(solution)/shard_map/ppermute | solution.py:270
  23.9 6.5 %collective-permute-start.9 = (f32[4,112,128]{2,1,0:T(8,128)S(1)}, f32[4,112,128]{2,1,0:T(8,128)S(1)}, u32[]{:S(2)}, u32[]{:S(2)}) collective-permute-start(f32[4,112,128]{2,1,0:T(8,128)S(1)} %get-tuple-element.41), channel_id=1, source_target_pairs={{0,4},{1,17},{2,6},{3,19},{4,0},{5,21},{6,2},{7,23},{8,12},{9,25},... | collective-permute-start | bytes 688136 | tf_op jit(solution)/shard_map/ppermute | solution.py:270
  30.4 10.7 %copy-start = (f32[13824]{0:T(1024)S(1)}, f32[13824]{0:T(1024)}, u32[]{:S(2)}) copy-start(f32[13824]{0:T(1024)} %param.11) | copy-start | bytes 165892
  30.4 10.8 %copy-start.1 = (f32[13824]{0:T(1024)S(1)}, f32[13824]{0:T(1024)}, u32[]{:S(2)}) copy-start(f32[13824]{0:T(1024)} %param.12) | copy-start | bytes 165892
  30.4 10.8 %copy-start.2 = (f32[13824]{0:T(1024)S(1)}, f32[13824]{0:T(1024)}, u32[]{:S(2)}) copy-start(f32[13824]{0:T(1024)} %param.13) | copy-start | bytes 165892
  30.4 5.2 %collective-permute-start.10 = (f32[1,112,128]{2,1,0:T(8,128)S(1)}, f32[1,112,128]{2,1,0:T(8,128)S(1)}, u32[]{:S(2)}, u32[]{:S(2)}) collective-permute-start(f32[1,112,128]{2,1,0:T(8,128)S(1)} %get-tuple-element.44), channel_id=1, source_target_pairs={{0,8},{1,5},{2,10},{3,7},{4,12},{5,1},{6,14},{7,3},{8,0},{9,13},{1... | collective-permute-start | bytes 172040 | tf_op jit(solution)/shard_map/ppermute | solution.py:270
  32.5 5.7 %collective-permute-start.11 = (f32[1,112,128]{2,1,0:T(8,128)S(1)}, f32[1,112,128]{2,1,0:T(8,128)S(1)}, u32[]{:S(2)}, u32[]{:S(2)}) collective-permute-start(f32[1,112,128]{2,1,0:T(8,128)S(1)} %get-tuple-element.45), channel_id=1, source_target_pairs={{0,16},{1,3},{2,18},{3,1},{4,20},{5,7},{6,22},{7,5},{8,24},{9,11},... | collective-permute-start | bytes 172040 | tf_op jit(solution)/shard_map/ppermute | solution.py:270
  35.1 6.0 %collective-permute-start.12 = (f32[1,112,128]{2,1,0:T(8,128)S(1)}, f32[1,112,128]{2,1,0:T(8,128)S(1)}, u32[]{:S(2)}, u32[]{:S(2)}) collective-permute-start(f32[1,112,128]{2,1,0:T(8,128)S(1)} %get-tuple-element.46), channel_id=1, source_target_pairs={{0,24},{1,7},{2,26},{3,5},{4,28},{5,3},{6,30},{7,1},{8,16},{9,15},... | collective-permute-start | bytes 172040 | tf_op jit(solution)/shard_map/ppermute | solution.py:270
  41.2 5.8 %collective-permute-start.15 = (bf16[1,112,128]{2,1,0:T(8,128)(2,1)S(1)}, bf16[1,112,128]{2,1,0:T(8,128)(2,1)S(1)}, u32[]{:S(2)}, u32[]{:S(2)}) collective-permute-start(bf16[1,112,128]{2,1,0:T(8,128)(2,1)S(1)} %shard_map.124.refs_7_.refs_0_), channel_id=1, source_target_pairs={{0,24},{1,25},{2,26},{3,27},{4,28},{5,29},{6,30},{7,31},{8,16},{9,... | collective-permute-start | bytes 86024 | tf_op jit(solution)/shard_map/ppermute | solution.py:270
  42.0 5.7 %collective-permute-start.14 = (bf16[1,112,128]{2,1,0:T(8,128)(2,1)S(1)}, bf16[1,112,128]{2,1,0:T(8,128)(2,1)S(1)}, u32[]{:S(2)}, u32[]{:S(2)}) collective-permute-start(bf16[1,112,128]{2,1,0:T(8,128)(2,1)S(1)} %shard_map.124.refs_7_.refs_0_), channel_id=1, source_target_pairs={{0,16},{1,17},{2,18},{3,19},{4,20},{5,21},{6,22},{7,23},{8,24},{9,... | collective-permute-start | bytes 86024 | tf_op jit(solution)/shard_map/ppermute | solution.py:270
  42.0 6.0 %collective-permute-start.13 = (bf16[1,112,128]{2,1,0:T(8,128)(2,1)S(1)}, bf16[1,112,128]{2,1,0:T(8,128)(2,1)S(1)}, u32[]{:S(2)}, u32[]{:S(2)}) collective-permute-start(bf16[1,112,128]{2,1,0:T(8,128)(2,1)S(1)} %shard_map.124.refs_7_.refs_0_), channel_id=1, source_target_pairs={{0,8},{1,9},{2,10},{3,11},{4,12},{5,13},{6,14},{7,15},{8,0},{9,1},... | collective-permute-start | bytes 86024 | tf_op jit(solution)/shard_map/ppermute | solution.py:270
  48.0 7.0 %collective-permute-start.20 = (bf16[4,112,128]{2,1,0:T(8,128)(2,1)S(1)}, bf16[4,112,128]{2,1,0:T(8,128)(2,1)S(1)}, u32[]{:S(2)}, u32[]{:S(2)}) collective-permute-start(bf16[4,112,128]{2,1,0:T(8,128)(2,1)S(1)} %shard_map.126.refs_0_), channel_id=1, source_target_pairs={{0,6},{1,7},{2,4},{3,5},{4,2},{5,3},{6,0},{7,1},{8,14},{9,15},{10,... | collective-permute-start | bytes 344072 | tf_op jit(solution)/shard_map/ppermute | solution.py:270
  49.4 6.9 %collective-permute-start.17 = (bf16[4,112,128]{2,1,0:T(8,128)(2,1)S(1)}, bf16[4,112,128]{2,1,0:T(8,128)(2,1)S(1)}, u32[]{:S(2)}, u32[]{:S(2)}) collective-permute-start(bf16[4,112,128]{2,1,0:T(8,128)(2,1)S(1)} %shard_map.126.refs_0_), channel_id=1, source_target_pairs={{0,4},{1,5},{2,6},{3,7},{4,0},{5,1},{6,2},{7,3},{8,12},{9,13},{10,... | collective-permute-start | bytes 344072 | tf_op jit(solution)/shard_map/ppermute | solution.py:270
  50.4 5.9 %collective-permute-start.16 = (bf16[4,112,128]{2,1,0:T(8,128)(2,1)S(1)}, bf16[4,112,128]{2,1,0:T(8,128)(2,1)S(1)}, u32[]{:S(2)}, u32[]{:S(2)}) collective-permute-start(bf16[4,112,128]{2,1,0:T(8,128)(2,1)S(1)} %shard_map.126.refs_0_), channel_id=1, source_target_pairs={{0,2},{1,3},{2,0},{3,1},{4,6},{5,7},{6,4},{7,5},{8,10},{9,11},{10,... | collective-permute-start | bytes 344072 | tf_op jit(solution)/shard_map/ppermute | solution.py:270
  51.6 5.2 %collective-permute-start.21 = (bf16[4,112,128]{2,1,0:T(8,128)(2,1)S(1)}, bf16[4,112,128]{2,1,0:T(8,128)(2,1)S(1)}, u32[]{:S(2)}, u32[]{:S(2)}) collective-permute-start(bf16[4,112,128]{2,1,0:T(8,128)(2,1)S(1)} %shard_map.126.refs_0_), channel_id=1, source_target_pairs={{0,1},{1,0},{2,3},{3,2},{4,5},{5,4},{6,7},{7,6},{8,9},{9,8},{10,11... | collective-permute-start | bytes 344072 | tf_op jit(solution)/shard_map/ppermute | solution.py:274
  55.0 1.8 %collective-permute-start.22 = (bf16[4,112,128]{2,1,0:T(8,128)(2,1)S(1)}, bf16[4,112,128]{2,1,0:T(8,128)(2,1)S(1)}, u32[]{:S(2)}, u32[]{:S(2)}) collective-permute-start(bf16[4,112,128]{2,1,0:T(8,128)(2,1)S(1)} %collective-permute-done.20.refs_1_), channel_id=1, source_target_pairs={{0,1},{1,0},{2,3},{3,2},{4,5},{5,4},{6,7},{7,6},{8,9},{9,8},{10,11... | collective-permute-start | bytes 344072 | tf_op jit(solution)/shard_map/ppermute | solution.py:274
  56.3 1.4 %collective-permute-start.19 = (bf16[4,112,128]{2,1,0:T(8,128)(2,1)S(1)}, bf16[4,112,128]{2,1,0:T(8,128)(2,1)S(1)}, u32[]{:S(2)}, u32[]{:S(2)}) collective-permute-start(bf16[4,112,128]{2,1,0:T(8,128)(2,1)S(1)} %collective-permute-done.17.refs_1_), channel_id=1, source_target_pairs={{0,1},{1,0},{2,3},{3,2},{4,5},{5,4},{6,7},{7,6},{8,9},{9,8},{10,11... | collective-permute-start | bytes 344072 | tf_op jit(solution)/shard_map/ppermute | solution.py:274
  56.3 1.5 %collective-permute-start.18 = (bf16[4,112,128]{2,1,0:T(8,128)(2,1)S(1)}, bf16[4,112,128]{2,1,0:T(8,128)(2,1)S(1)}, u32[]{:S(2)}, u32[]{:S(2)}) collective-permute-start(bf16[4,112,128]{2,1,0:T(8,128)(2,1)S(1)} %collective-permute-done.16.refs_0_), channel_id=1, source_target_pairs={{0,1},{1,0},{2,3},{3,2},{4,5},{5,4},{6,7},{7,6},{8,9},{9,8},{10,11... | collective-permute-start | bytes 344072 | tf_op jit(solution)/shard_map/ppermute | solution.py:274
where the time goes:
time: 58.8 us; the launch traced here: 58.6 us
  starting transfers between devices  26.5 us (45%)
  waiting for transfers between devices  21.7 us (37%)
  Pallas kernels  8.43 us (14%)
  other arithmetic  1.24 us (2%)
  between operations  0.79 us (1%)
    ppermute x12, starting transfers between devices, swap(): return lax.ppermute(array, AXES, pairs)  17.6 us
    ppermute x12, waiting for transfers between devices, swap(): return lax.ppermute(array, AXES, pairs)  15.2 us
    ppermute x4, starting transfers between devices, neighbours(): move = lambda array, pairs: lax.ppermute(array, 'depth', pairs)  7.72 us
    ppermute x4, waiting for transfers between devices, neighbours(): move = lambda array, pairs: lax.ppermute(array, 'depth', pairs)  4.46 us
    pallas_call x1, Pallas kernels, staged(): call(functools.partial(input_body, width), (b16(*act.shape), f32(8, chans...  2.95 us
    ppermute x7, waiting for transfers between devices, swap_cores(): return lax.ppermute(array, 'samp', [(0, 1), (1, 0)])  2.01 us
    pallas_call x2, Pallas kernels, place(): pl.pallas_call(functools.partial(place_body, n, size, groups), out_shape=...  1.66 us
    convert_element_type x1, other arithmetic, cotangent(): (out_grad.reshape(-1, chans)[part].astype(jnp.float32) * slope).astype(jn...  1.24 us
  transfers between devices with their start and end apart: 23, of which 15 were waited for; matrix products, arithmetic and copies ran while one was open for 0% of the time, Pallas kernels for 11%

commit v1 on v0

--- a/solution.py
+++ b/solution.py
@@ -152,9 +152,28 @@
     token[...] = jnp.zeros(token.shape, token.dtype)
 
 
+def add_split(odd, terms, sums):
+    side, count = terms[2].shape[0], terms[4].shape[0]
+    low, high = side + 1, side + 1 + count
+    for piece in range(sums.shape[0]):
+        if low <= piece < high:
+            pair, index = 4, piece - low
+        elif piece in (side, high):
+            pair, index = 0, side + (piece == high)
+        else:
+            upper = piece > high
+            pair, index = (2 if upper == odd else 0), piece - upper * (high + 1)
+        sums[piece] = terms[pair][index] + terms[pair + 1][index]
+
+
 def merge_body(n, stage, swapped, split, core, first, second, *refs):
-    outs = refs[len(refs) - n :]
-    terms = [r for r in refs[: len(refs) - n] if len(r.shape) == 3]
+    end = len(refs) - split
+    outs = refs[end - n : end]
+    terms = [r for r in refs[: end - n] if len(r.shape) == 3]
+    if split:
+        for odd in range(2):
+            pl.when((first[0] & 1) == odd)(functools.partial(add_split, odd, terms, refs[-1]))
+        terms = [refs[-1]]
     flip = core[0] != swapped
     own = jnp.where(flip, second[0], first[0])
     group, other = jnp.where(flip, n, 1), jnp.where(flip, 1, n)
@@ -162,24 +181,7 @@
         at = own ^ jnp.where(core[0] == 0, *masks)
         for h in range(outs[j].shape[0]):
             piece = at * group + h * other if outs[j].shape[0] > 1 else at
-            if not split:
-                outs[j][h] = functools.reduce(lambda x, y: x + y, [term[piece] for term in terms])
-                continue
-            side, count = terms[2].shape[0], terms[4].shape[0]
-            low, high = side + 1, side + 1 + count
-            inner = (piece >= low) & (piece < high)
-            upper = (piece > high).astype(jnp.int32)
-            outer = jnp.clip(piece - upper * (high + 1), 0, side - 1)
-            across = (piece == side) | (piece == high)
-            near = (upper == (first[0] & 1)) & jnp.logical_not(across | inner)
-            late = jnp.where(across, side + (piece == high).astype(jnp.int32), outer)
-            early = jnp.clip(piece - low, 0, count - 1)
-            rest = jnp.logical_not(inner | near)
-            for chosen, pair, index in ((inner, 4, early), (near, 2, outer), (rest, 0, late)):
-
-                @pl.when(chosen)
-                def _(out=outs[j], pair=pair, index=index, h=h):
-                    out[h] = terms[pair][index] + terms[pair + 1][index]
+            outs[j][h] = functools.reduce(lambda x, y: x + y, [term[piece] for term in terms])
 
 
 def adam_step(count, core, terms, master, moment, second):
@@ -321,7 +323,7 @@
     late_come = swap_cores(sent)
     terms = (late, late_come, near, near_come, early, early_come)
     parts = call(
-        functools.partial(merge_body, n, "first", 0, True), (f32(n, wide, chans),) * n, 6, scalars=3
+        functools.partial(merge_body, n, "first", 0, True), (f32(n, wide, chans),) * n, 6, scalars=3, scratch=[pltpu.VMEM((pieces, wide, chans), jnp.float32)]
     )(core, first, second, *terms)
     got = exchange("first", n, parts, (1, n))
     grad_input, token = call(

time: 58.8 us -> 58.6 us (level)
  no operation moved by 1% of the time
where the time goes in v1:
time: 58.6 us; the launch traced here: 58.4 us
  starting transfers between devices  26.5 us (45%)
  waiting for transfers between devices  21.7 us (37%)
  Pallas kernels  8.2 us (14%)
  other arithmetic  1.24 us (2%)
  between operations  0.79 us (1%)
    ppermute x12, starting transfers between devices, swap(): return lax.ppermute(array, AXES, pairs)  17.6 us
    ppermute x12, waiting for transfers between devices, swap(): return lax.ppermute(array, AXES, pairs)  15.2 us
    ppermute x4, starting transfers between devices, neighbours(): move = lambda array, pairs: lax.ppermute(array, 'depth', pairs)  7.72 us
    ppermute x4, waiting for transfers between devices, neighbours(): move = lambda array, pairs: lax.ppermute(array, 'depth', pairs)  4.46 us
    pallas_call x1, Pallas kernels, staged(): call(functools.partial(input_body, width), (b16(*act.shape), f32(8, chans...  2.95 us
    ppermute x7, waiting for transfers between devices, swap_cores(): return lax.ppermute(array, 'samp', [(0, 1), (1, 0)])  2.01 us
    pallas_call x2, Pallas kernels, place(): pl.pallas_call(functools.partial(place_body, n, size, groups), out_shape=...  1.66 us
    convert_element_type x1, other arithmetic, cotangent(): (out_grad.reshape(-1, chans)[part].astype(jnp.float32) * slope).astype(jn...  1.24 us
  transfers between devices with their start and end apart: 23, of which 15 were waited for; matrix products, arithmetic and copies ran while one was open for 0% of the time, Pallas kernels for 11%

profile of v1, /device:TPU:0, one launch (start us, length us, event | category | flops | bytes accessed | tf_op | source)
XLA Modules:
  0.0 58.4 jit_solution(2121990731986008817)
XLA Ops:
  0.6 1.2 %multiply_convert_fusion = (bf16[1,1,32,16,128]{4,3,2,1,0:T(8,128)(2,1)S(1)}, bf16[1,1,32,16,128]{4,3,2,1,0:T(8,128)(2,1)S(1)}) fusion(bf16[1,1,64,16,128]{4,3,2,1,0:T(8,128)(2,1)} %param.8, bf16[1,1,64,16,128]{4,3,2,1,0:T(8,128)(2,1)} %param.9), kind=kLoop, calls=%fused_computation | loop fusion | flops 655360 | bytes 786432 | tf_op jit(solution)/shard_map/convert_element_type | solution.py:425
  1.9 3.0 %collective-permute-start = (bf16[512,128]{1,0:T(8,128)(2,1)S(1)}, bf16[512,128]{1,0:T(8,128)(2,1)S(1)}, u32[]{:S(2)}, u32[]{:S(2)}) collective-permute-start(bf16[512,128]{1,0:T(8,128)(2,1)S(1)} %bitcast.27), channel_id=1, source_target_pairs={{0,2},{2,0},{4,6},{6,4},{8,10},{10,8},{12,14},{14,12},{16,18},{18,... | collective-permute-start | bytes 393224 | tf_op jit(solution)/shard_map/ppermute | solution.py:406
  5.0 0.7 %collective-permute-start.3 = (bf16[512,128]{1,0:T(8,128)(2,1)S(1)}, bf16[512,128]{1,0:T(8,128)(2,1)S(1)}, u32[]{:S(2)}, u32[]{:S(2)}) collective-permute-start(bf16[512,128]{1,0:T(8,128)(2,1)S(1)} %bitcast.24), channel_id=1, source_target_pairs={{2,4},{6,8},{10,12},{14,16},{18,20},{22,24},{26,28},{4,2},{8,6},{1... | collective-permute-start | bytes 393224 | tf_op jit(solution)/shard_map/ppermute | solution.py:406
  5.7 3.6 %collective-permute-done.refs_2_.top = bf16[512,128]{1,0:T(8,128)(2,1)S(1)} collective-permute-done((bf16[512,128]{1,0:T(8,128)(2,1)S(1)}, bf16[512,128]{1,0:T(8,128)(2,1)S(1)}, u32[]{:S(2)}, u32[]{:S(2)}) %collective-permute-start) | collective-permute-done | bytes 131104 | tf_op jit(solution)/shard_map/ppermute | solution.py:406
  9.3 3.9 %collective-permute-start.2 = (bf16[512,128]{1,0:T(8,128)(2,1)S(1)}, bf16[512,128]{1,0:T(8,128)(2,1)S(1)}, u32[]{:S(2)}, u32[]{:S(2)}) collective-permute-start(bf16[512,128]{1,0:T(8,128)(2,1)S(1)} %collective-permute-done.refs_2_.top), channel_id=1, source_target_pairs={{0,4},{4,8},{8,12},{12,16},{16,20},{20,24},{24,28},{6,2},{10,6},{1... | collective-permute-start | bytes 393224 | tf_op jit(solution)/shard_map/ppermute | solution.py:406
  13.2 0.8 %shard_map.119 = (f32[288,128]{1,0:T(8,128)S(1)}, f32[4,112,128]{2,1,0:T(8,128)S(1)}, f32[4,112,128]{2,1,0:T(8,128)S(1)}) custom-call(s32[1]{0:T(128)} %bitcast.5.core.me, bf16[1024,128]{1,0:T(8,128)(2,1)S(1)} %bitcast.31, bf16[512,128]{1,0:T(8,128)(2,1)S(1)} %bitcast.28, bf16[512,128]{1,0:T(8,128)(2,1)S(1)} %bitcast.25), custom_call_target="tpu_custom_call" | custom-call | flops 301989888 | tf_op jit(solution)/shard_map/pallas_call | solution.py:301
  14.1 0.9 %shard_map.120 = (f32[72,128]{1,0:T(8,128)S(1)}, f32[5,112,128]{2,1,0:T(8,128)S(1)}, f32[5,112,128]{2,1,0:T(8,128)S(1)}) custom-call(s32[1]{0:T(128)} %bitcast.5.core.me, s32[1]{0:T(128)} %bitcast.odd, bf16[1024,128]{1,0:T(8,128)(2,1)S(1)} %bitcast.32, bf16[512,128]{1,0:T(8,128)(2,1)S(1)} %collective-permute-done.refs_2_.top, ...), custom_call_target="tpu_custom_call" | custom-call | flops 301989888 | tf_op jit(solution)/shard_map/pallas_call | solution.py:308
  15.0 0.8 %collective-permute-done.2.refs_4_.top = bf16[512,128]{1,0:T(8,128)(2,1)S(1)} collective-permute-done((bf16[512,128]{1,0:T(8,128)(2,1)S(1)}, bf16[512,128]{1,0:T(8,128)(2,1)S(1)}, u32[]{:S(2)}, u32[]{:S(2)}) %collective-permute-start.2) | collective-permute-done | bytes 131104 | tf_op jit(solution)/shard_map/ppermute | solution.py:406
  15.8 0.9 %shard_map.121 = (f32[7,112,128]{2,1,0:T(8,128)S(1)}, f32[7,112,128]{2,1,0:T(8,128)S(1)}) custom-call(s32[1]{0:T(128)} %bitcast.5.core.me, s32[1]{0:T(128)} %bitcast.odd, bf16[1024,128]{1,0:T(8,128)(2,1)S(1)} %bitcast.33, bf16[512,128]{1,0:T(8,128)(2,1)S(1)} %collective-permute-done.2.refs_4_.top, ...), custom_call_target="tpu_custom_call" | custom-call | flops 301989888 | tf_op jit(solution)/shard_map/pallas_call | solution.py:316
  17.4 1.9 %collective-permute-done.6.refs_5_ = f32[4,112,128]{2,1,0:T(8,128)S(1)} collective-permute-done((f32[4,112,128]{2,1,0:T(8,128)S(1)}, f32[4,112,128]{2,1,0:T(8,128)S(1)}, u32[]{:S(2)}, u32[]{:S(2)}) %collective-permute-start.6) | collective-permute-done | bytes 229408 | tf_op jit(solution)/shard_map/ppermute | solution.py:276
  19.5 4.2 %collective-permute-start.7 = (f32[4,112,128]{2,1,0:T(8,128)S(1)}, f32[4,112,128]{2,1,0:T(8,128)S(1)}, u32[]{:S(2)}, u32[]{:S(2)}) collective-permute-start(f32[4,112,128]{2,1,0:T(8,128)S(1)} %get-tuple-element.39), channel_id=1, source_target_pairs={{0,6},{1,25},{2,4},{3,27},{4,2},{5,29},{6,0},{7,31},{8,14},{9,17},... | collective-permute-start | bytes 688136 | tf_op jit(solution)/shard_map/ppermute | solution.py:272
  23.7 0.6 %collective-permute-start.9 = (f32[4,112,128]{2,1,0:T(8,128)S(1)}, f32[4,112,128]{2,1,0:T(8,128)S(1)}, u32[]{:S(2)}, u32[]{:S(2)}) collective-permute-start(f32[4,112,128]{2,1,0:T(8,128)S(1)} %get-tuple-element.41), channel_id=1, source_target_pairs={{0,4},{1,17},{2,6},{3,19},{4,0},{5,21},{6,2},{7,23},{8,12},{9,25},... | collective-permute-start | bytes 688136 | tf_op jit(solution)/shard_map/ppermute | solution.py:272
  24.3 3.0 %shard_map.118 = (bf16[1024,128]{1,0:T(8,128)(2,1)}, f32[8,128]{1,0:T(8,128)S(1)}) custom-call(s32[1]{0:T(128)} %bitcast.odd, bf16[27,128,128]{2,1,0:T(8,128)(2,1)S(1)} %bitcast.30, bf16[512,128]{1,0:T(8,128)(2,1)S(1)} %bitcast.29, bf16[512,128]{1,0:T(8,128)(2,1)S(1)} %bitcast.26, bf16[512,128]{1,0:T(8,128)(2,1)S(1)} %collective-permute-done.refs_2_.top, ...), custom_call_target="tpu_custom_call" | custom-call | flops 905969664 | bytes 4194304 | tf_op jit(solution)/shard_map/pallas_call | solution.py:329
  27.7 2.2 %collective-permute-done.8.refs_2_ = f32[4,112,128]{2,1,0:T(8,128)S(1)} collective-permute-done((f32[4,112,128]{2,1,0:T(8,128)S(1)}, f32[4,112,128]{2,1,0:T(8,128)S(1)}, u32[]{:S(2)}, u32[]{:S(2)}) %collective-permute-start.8) | collective-permute-done | bytes 229408 | tf_op jit(solution)/shard_map/ppermute | solution.py:272
  30.2 2.1 %collective-permute-start.10 = (f32[1,112,128]{2,1,0:T(8,128)S(1)}, f32[1,112,128]{2,1,0:T(8,128)S(1)}, u32[]{:S(2)}, u32[]{:S(2)}) collective-permute-start(f32[1,112,128]{2,1,0:T(8,128)S(1)} %get-tuple-element.44), channel_id=1, source_target_pairs={{0,8},{1,5},{2,10},{3,7},{4,12},{5,1},{6,14},{7,3},{8,0},{9,13},{1... | collective-permute-start | bytes 172040 | tf_op jit(solution)/shard_map/ppermute | solution.py:272
  32.3 2.6 %collective-permute-start.11 = (f32[1,112,128]{2,1,0:T(8,128)S(1)}, f32[1,112,128]{2,1,0:T(8,128)S(1)}, u32[]{:S(2)}, u32[]{:S(2)}) collective-permute-start(f32[1,112,128]{2,1,0:T(8,128)S(1)} %get-tuple-element.45), channel_id=1, source_target_pairs={{0,16},{1,3},{2,18},{3,1},{4,20},{5,7},{6,22},{7,5},{8,24},{9,11},... | collective-permute-start | bytes 172040 | tf_op jit(solution)/shard_map/ppermute | solution.py:272
  34.9 0.5 collective-permute-done.10.refs_1_
  35.4 2.6 %collective-permute-done.11.refs_2_ = f32[1,112,128]{2,1,0:T(8,128)S(1)} collective-permute-done((f32[1,112,128]{2,1,0:T(8,128)S(1)}, f32[1,112,128]{2,1,0:T(8,128)S(1)}, u32[]{:S(2)}, u32[]{:S(2)}) %collective-permute-start.11) | collective-permute-done | bytes 57376 | tf_op jit(solution)/shard_map/ppermute | solution.py:272
  38.0 2.9 %collective-permute-done.12.refs_3_ = f32[1,112,128]{2,1,0:T(8,128)S(1)} collective-permute-done((f32[1,112,128]{2,1,0:T(8,128)S(1)}, f32[1,112,128]{2,1,0:T(8,128)S(1)}, u32[]{:S(2)}, u32[]{:S(2)}) %collective-permute-start.12) | collective-permute-done | bytes 57376 | tf_op jit(solution)/shard_map/ppermute | solution.py:272
  41.0 0.8 %collective-permute-start.15 = (bf16[1,112,128]{2,1,0:T(8,128)(2,1)S(1)}, bf16[1,112,128]{2,1,0:T(8,128)(2,1)S(1)}, u32[]{:S(2)}, u32[]{:S(2)}) collective-permute-start(bf16[1,112,128]{2,1,0:T(8,128)(2,1)S(1)} %shard_map.124.refs_7_.refs_0_), channel_id=1, source_target_pairs={{0,24},{1,25},{2,26},{3,27},{4,28},{5,29},{6,30},{7,31},{8,16},{9,... | collective-permute-start | bytes 86024 | tf_op jit(solution)/shard_map/ppermute | solution.py:272
  41.8 3.7 %collective-permute-start.13 = (bf16[1,112,128]{2,1,0:T(8,128)(2,1)S(1)}, bf16[1,112,128]{2,1,0:T(8,128)(2,1)S(1)}, u32[]{:S(2)}, u32[]{:S(2)}) collective-permute-start(bf16[1,112,128]{2,1,0:T(8,128)(2,1)S(1)} %shard_map.124.refs_7_.refs_0_), channel_id=1, source_target_pairs={{0,8},{1,9},{2,10},{3,11},{4,12},{5,13},{6,14},{7,15},{8,0},{9,1},... | collective-permute-start | bytes 86024 | tf_op jit(solution)/shard_map/ppermute | solution.py:272
  45.4 0.7 %shard_map.125 = (f32[108,128]{1,0:T(8,128)}, f32[108,128]{1,0:T(8,128)}, f32[108,128]{1,0:T(8,128)}, f32[108,128]{1,0:T(8,128)}, f32[8,128]{1,0:T(8,128)S(1)}) custom-call(s32[1]{0:T(128)} %bitcast.5.core.me, f32[1,112,128]{2,1,0:T(8,128)S(1)} %get-tuple-element.43.refs_0_, f32[1,112,128]{2,1,0:T(8,128)S(1)} %collective-permute-done.10.refs_1_, ...), custom_call_target="tpu_custom_call" | custom-call | tf_op jit(solution)/shard_map/pallas_call | solution.py:349
  46.1 0.6 %collective-permute-done.15.refs_3_ = bf16[1,112,128]{2,1,0:T(8,128)(2,1)S(1)} collective-permute-done((bf16[1,112,128]{2,1,0:T(8,128)(2,1)S(1)}, bf16[1,112,128]{2,1,0:T(8,128)(2,1)S(1)}, u32[]{:S(2)}, u32[]{:S(2)}) %collective-permute-start.15) | collective-permute-done | bytes 28704 | tf_op jit(solution)/shard_map/ppermute | solution.py:272
  46.7 0.7 %collective-permute-done.14.refs_2_ = bf16[1,112,128]{2,1,0:T(8,128)(2,1)S(1)} collective-permute-done((bf16[1,112,128]{2,1,0:T(8,128)(2,1)S(1)}, bf16[1,112,128]{2,1,0:T(8,128)(2,1)S(1)}, u32[]{:S(2)}, u32[]{:S(2)}) %collective-permute-start.14) | collective-permute-done | bytes 28704 | tf_op jit(solution)/shard_map/ppermute | solution.py:272
  47.8 1.4 %collective-permute-start.20 = (bf16[4,112,128]{2,1,0:T(8,128)(2,1)S(1)}, bf16[4,112,128]{2,1,0:T(8,128)(2,1)S(1)}, u32[]{:S(2)}, u32[]{:S(2)}) collective-permute-start(bf16[4,112,128]{2,1,0:T(8,128)(2,1)S(1)} %shard_map.126.refs_0_), channel_id=1, source_target_pairs={{0,6},{1,7},{2,4},{3,5},{4,2},{5,3},{6,0},{7,1},{8,14},{9,15},{10,... | collective-permute-start | bytes 344072 | tf_op jit(solution)/shard_map/ppermute | solution.py:272
  49.2 1.0 %collective-permute-start.17 = (bf16[4,112,128]{2,1,0:T(8,128)(2,1)S(1)}, bf16[4,112,128]{2,1,0:T(8,128)(2,1)S(1)}, u32[]{:S(2)}, u32[]{:S(2)}) collective-permute-start(bf16[4,112,128]{2,1,0:T(8,128)(2,1)S(1)} %shard_map.126.refs_0_), channel_id=1, source_target_pairs={{0,4},{1,5},{2,6},{3,7},{4,0},{5,1},{6,2},{7,3},{8,12},{9,13},{10,... | collective-permute-start | bytes 344072 | tf_op jit(solution)/shard_map/ppermute | solution.py:272
  50.2 1.1 %collective-permute-start.16 = (bf16[4,112,128]{2,1,0:T(8,128)(2,1)S(1)}, bf16[4,112,128]{2,1,0:T(8,128)(2,1)S(1)}, u32[]{:S(2)}, u32[]{:S(2)}) collective-permute-start(bf16[4,112,128]{2,1,0:T(8,128)(2,1)S(1)} %shard_map.126.refs_0_), channel_id=1, source_target_pairs={{0,2},{1,3},{2,0},{3,1},{4,6},{5,7},{6,4},{7,5},{8,10},{9,11},{10,... | collective-permute-start | bytes 344072 | tf_op jit(solution)/shard_map/ppermute | solution.py:272
  51.4 3.4 %collective-permute-done.20.refs_1_ = bf16[4,112,128]{2,1,0:T(8,128)(2,1)S(1)} collective-permute-done((bf16[4,112,128]{2,1,0:T(8,128)(2,1)S(1)}, bf16[4,112,128]{2,1,0:T(8,128)(2,1)S(1)}, u32[]{:S(2)}, u32[]{:S(2)}) %collective-permute-start.20) | collective-permute-done | bytes 114720 | tf_op jit(solution)/shard_map/ppermute | solution.py:272
  54.8 1.3 %collective-permute-done.17.refs_1_ = bf16[4,112,128]{2,1,0:T(8,128)(2,1)S(1)} collective-permute-done((bf16[4,112,128]{2,1,0:T(8,128)(2,1)S(1)}, bf16[4,112,128]{2,1,0:T(8,128)(2,1)S(1)}, u32[]{:S(2)}, u32[]{:S(2)}) %collective-permute-start.17) | collective-permute-done | bytes 114720 | tf_op jit(solution)/shard_map/ppermute | solution.py:272
  56.1 0.5 collective-permute-start.18
  56.6 0.8 %shard_map.127.refs_4_ = bf16[3456,128]{1,0:T(8,128)(2,1)} custom-call(s32[1]{0:T(128)} %bitcast.5.core.me, s32[1]{0:T(128)} %bitcast.6.first, s32[1]{0:T(128)} %bitcast.7.second, bf16[4,112,128]{2,1,0:T(8,128)(2,1)S(1)} %shard_map.126.refs_0_, bf16[4,112,128]{2,1,0:T(8,128)(2,1)S(1)} %collective-permute-done.20.refs_1_, ...), custom_call_target="tpu_custom_call" | custom-call | tf_op jit(solution)/shard_map/pallas_call | solution.py:254
  57.5 0.8 %shard_map.128 = bf16[3456,128]{1,0:T(8,128)(2,1)} custom-call(s32[1]{0:T(128)} %bitcast.5.core.me, s32[1]{0:T(128)} %bitcast.6.first, s32[1]{0:T(128)} %bitcast.7.second, bf16[4,112,128]{2,1,0:T(8,128)(2,1)S(1)} %collective-permute-done.16.refs_0_, bf16[4,112,128]{2,1,0:T(8,128)(2,1)S(1)} %collective-permute-done.17.refs_1_, ...), custom_call_target="tpu_custom_call", output_to_operand_aliasing={{}: (7, {})} | custom-call | tf_op jit(solution)/shard_map/pallas_call | solution.py:254
  (36 shorter events, 2.2 us)
Async XLA Ops:
  0.6 12.6 %copy-start.4 = (bf16[1,1,64,16,128]{4,3,2,1,0:T(8,128)(2,1)S(1)}, bf16[1,1,64,16,128]{4,3,2,1,0:T(8,128)(2,1)}, u32[]{:S(2)}) copy-start(bf16[1,1,64,16,128]{4,3,2,1,0:T(8,128)(2,1)} %param.7) | copy-start | bytes 786436
  1.9 7.4 %collective-permute-start = (bf16[512,128]{1,0:T(8,128)(2,1)S(1)}, bf16[512,128]{1,0:T(8,128)(2,1)S(1)}, u32[]{:S(2)}, u32[]{:S(2)}) collective-permute-start(bf16[512,128]{1,0:T(8,128)(2,1)S(1)} %bitcast.27), channel_id=1, source_target_pairs={{0,2},{2,0},{4,6},{6,4},{8,10},{10,8},{12,14},{14,12},{16,18},{18,... | collective-permute-start | bytes 393224 | tf_op jit(solution)/shard_map/ppermute | solution.py:406
  4.9 9.2 %collective-permute-start.1 = (bf16[512,128]{1,0:T(8,128)(2,1)S(1)}, bf16[512,128]{1,0:T(8,128)(2,1)S(1)}, u32[]{:S(2)}, u32[]{:S(2)}) collective-permute-start(bf16[512,128]{1,0:T(8,128)(2,1)S(1)} %bitcast.23), channel_id=1, source_target_pairs={{0,2},{2,0},{4,6},{6,4},{8,10},{10,8},{12,14},{14,12},{16,18},{18,... | collective-permute-start | bytes 393224 | tf_op jit(solution)/shard_map/ppermute | solution.py:406
  5.0 10.0 %collective-permute-start.3 = (bf16[512,128]{1,0:T(8,128)(2,1)S(1)}, bf16[512,128]{1,0:T(8,128)(2,1)S(1)}, u32[]{:S(2)}, u32[]{:S(2)}) collective-permute-start(bf16[512,128]{1,0:T(8,128)(2,1)S(1)} %bitcast.24), channel_id=1, source_target_pairs={{2,4},{6,8},{10,12},{14,16},{18,20},{22,24},{26,28},{4,2},{8,6},{1... | collective-permute-start | bytes 393224 | tf_op jit(solution)/shard_map/ppermute | solution.py:406
  9.3 6.6 %collective-permute-start.2 = (bf16[512,128]{1,0:T(8,128)(2,1)S(1)}, bf16[512,128]{1,0:T(8,128)(2,1)S(1)}, u32[]{:S(2)}, u32[]{:S(2)}) collective-permute-start(bf16[512,128]{1,0:T(8,128)(2,1)S(1)} %collective-permute-done.refs_2_.top), channel_id=1, source_target_pairs={{0,4},{4,8},{8,12},{12,16},{16,20},{20,24},{24,28},{6,2},{10,6},{1... | collective-permute-start | bytes 393224 | tf_op jit(solution)/shard_map/ppermute | solution.py:406
  16.7 2.5 %collective-permute-start.4 = (f32[7,112,128]{2,1,0:T(8,128)S(1)}, f32[7,112,128]{2,1,0:T(8,128)S(1)}, u32[]{:S(2)}, u32[]{:S(2)}) collective-permute-start(f32[7,112,128]{2,1,0:T(8,128)S(1)} %get-tuple-element.33), channel_id=1, source_target_pairs={{0,1},{1,0},{2,3},{3,2},{4,5},{5,4},{6,7},{7,6},{8,9},{9,8},{10,11... | collective-permute-start | bytes 1204232 | tf_op jit(solution)/shard_map/ppermute | solution.py:276
  16.8 2.5 %collective-permute-start.5 = (f32[5,112,128]{2,1,0:T(8,128)S(1)}, f32[5,112,128]{2,1,0:T(8,128)S(1)}, u32[]{:S(2)}, u32[]{:S(2)}) collective-permute-start(f32[5,112,128]{2,1,0:T(8,128)S(1)} %get-tuple-element.35), channel_id=1, source_target_pairs={{0,1},{1,0},{2,3},{3,2},{4,5},{5,4},{6,7},{7,6},{8,9},{9,8},{10,11... | collective-permute-start | bytes 860168 | tf_op jit(solution)/shard_map/ppermute | solution.py:276
  17.3 2.0 %collective-permute-start.6 = (f32[4,112,128]{2,1,0:T(8,128)S(1)}, f32[4,112,128]{2,1,0:T(8,128)S(1)}, u32[]{:S(2)}, u32[]{:S(2)}) collective-permute-start(f32[4,112,128]{2,1,0:T(8,128)S(1)} %get-tuple-element.37), channel_id=1, source_target_pairs={{0,1},{1,0},{2,3},{3,2},{4,5},{5,4},{6,7},{7,6},{8,9},{9,8},{10,11... | collective-permute-start | bytes 688136 | tf_op jit(solution)/shard_map/ppermute | solution.py:276
  19.2 5.1 %copy-start.3 = (bf16[3,3,3,128,128]{4,3,2,1,0:T(8,128)(2,1)S(1)}, bf16[3,3,3,128,128]{4,3,2,1,0:T(8,128)(2,1)}, u32[]{:S(2)}) copy-start(bf16[3,3,3,128,128]{4,3,2,1,0:T(8,128)(2,1)} %param.10) | copy-start | bytes 2654212
  19.5 8.3 %collective-permute-start.7 = (f32[4,112,128]{2,1,0:T(8,128)S(1)}, f32[4,112,128]{2,1,0:T(8,128)S(1)}, u32[]{:S(2)}, u32[]{:S(2)}) collective-permute-start(f32[4,112,128]{2,1,0:T(8,128)S(1)} %get-tuple-element.39), channel_id=1, source_target_pairs={{0,6},{1,25},{2,4},{3,27},{4,2},{5,29},{6,0},{7,31},{8,14},{9,17},... | collective-permute-start | bytes 688136 | tf_op jit(solution)/shard_map/ppermute | solution.py:272
  23.7 6.2 %collective-permute-start.8 = (f32[4,112,128]{2,1,0:T(8,128)S(1)}, f32[4,112,128]{2,1,0:T(8,128)S(1)}, u32[]{:S(2)}, u32[]{:S(2)}) collective-permute-start(f32[4,112,128]{2,1,0:T(8,128)S(1)} %get-tuple-element.40), channel_id=1, source_target_pairs={{0,2},{1,9},{2,0},{3,11},{4,6},{5,13},{6,4},{7,15},{8,10},{9,1},{1... | collective-permute-start | bytes 688136 | tf_op jit(solution)/shard_map/ppermute | solution.py:272
  23.7 6.5 %collective-permute-start.9 = (f32[4,112,128]{2,1,0:T(8,128)S(1)}, f32[4,112,128]{2,1,0:T(8,128)S(1)}, u32[]{:S(2)}, u32[]{:S(2)}) collective-permute-start(f32[4,112,128]{2,1,0:T(8,128)S(1)} %get-tuple-element.41), channel_id=1, source_target_pairs={{0,4},{1,17},{2,6},{3,19},{4,0},{5,21},{6,2},{7,23},{8,12},{9,25},... | collective-permute-start | bytes 688136 | tf_op jit(solution)/shard_map/ppermute | solution.py:272
  30.1 10.7 %copy-start = (f32[13824]{0:T(1024)S(1)}, f32[13824]{0:T(1024)}, u32[]{:S(2)}) copy-start(f32[13824]{0:T(1024)} %param.11) | copy-start | bytes 165892
  30.1 10.7 %copy-start.1 = (f32[13824]{0:T(1024)S(1)}, f32[13824]{0:T(1024)}, u32[]{:S(2)}) copy-start(f32[13824]{0:T(1024)} %param.12) | copy-start | bytes 165892
  30.1 10.8 %copy-start.2 = (f32[13824]{0:T(1024)S(1)}, f32[13824]{0:T(1024)}, u32[]{:S(2)}) copy-start(f32[13824]{0:T(1024)} %param.13) | copy-start | bytes 165892
  30.2 5.2 %collective-permute-start.10 = (f32[1,112,128]{2,1,0:T(8,128)S(1)}, f32[1,112,128]{2,1,0:T(8,128)S(1)}, u32[]{:S(2)}, u32[]{:S(2)}) collective-permute-start(f32[1,112,128]{2,1,0:T(8,128)S(1)} %get-tuple-element.44), channel_id=1, source_target_pairs={{0,8},{1,5},{2,10},{3,7},{4,12},{5,1},{6,14},{7,3},{8,0},{9,13},{1... | collective-permute-start | bytes 172040 | tf_op jit(solution)/shard_map/ppermute | solution.py:272
  32.3 5.7 %collective-permute-start.11 = (f32[1,112,128]{2,1,0:T(8,128)S(1)}, f32[1,112,128]{2,1,0:T(8,128)S(1)}, u32[]{:S(2)}, u32[]{:S(2)}) collective-permute-start(f32[1,112,128]{2,1,0:T(8,128)S(1)} %get-tuple-element.45), channel_id=1, source_target_pairs={{0,16},{1,3},{2,18},{3,1},{4,20},{5,7},{6,22},{7,5},{8,24},{9,11},... | collective-permute-start | bytes 172040 | tf_op jit(solution)/shard_map/ppermute | solution.py:272
  34.9 6.0 %collective-permute-start.12 = (f32[1,112,128]{2,1,0:T(8,128)S(1)}, f32[1,112,128]{2,1,0:T(8,128)S(1)}, u32[]{:S(2)}, u32[]{:S(2)}) collective-permute-start(f32[1,112,128]{2,1,0:T(8,128)S(1)} %get-tuple-element.46), channel_id=1, source_target_pairs={{0,24},{1,7},{2,26},{3,5},{4,28},{5,3},{6,30},{7,1},{8,16},{9,15},... | collective-permute-start | bytes 172040 | tf_op jit(solution)/shard_map/ppermute | solution.py:272
  41.0 5.8 %collective-permute-start.15 = (bf16[1,112,128]{2,1,0:T(8,128)(2,1)S(1)}, bf16[1,112,128]{2,1,0:T(8,128)(2,1)S(1)}, u32[]{:S(2)}, u32[]{:S(2)}) collective-permute-start(bf16[1,112,128]{2,1,0:T(8,128)(2,1)S(1)} %shard_map.124.refs_7_.refs_0_), channel_id=1, source_target_pairs={{0,24},{1,25},{2,26},{3,27},{4,28},{5,29},{6,30},{7,31},{8,16},{9,... | collective-permute-start | bytes 86024 | tf_op jit(solution)/shard_map/ppermute | solution.py:272
  41.7 5.7 %collective-permute-start.14 = (bf16[1,112,128]{2,1,0:T(8,128)(2,1)S(1)}, bf16[1,112,128]{2,1,0:T(8,128)(2,1)S(1)}, u32[]{:S(2)}, u32[]{:S(2)}) collective-permute-start(bf16[1,112,128]{2,1,0:T(8,128)(2,1)S(1)} %shard_map.124.refs_7_.refs_0_), channel_id=1, source_target_pairs={{0,16},{1,17},{2,18},{3,19},{4,20},{5,21},{6,22},{7,23},{8,24},{9,... | collective-permute-start | bytes 86024 | tf_op jit(solution)/shard_map/ppermute | solution.py:272
  41.8 6.0 %collective-permute-start.13 = (bf16[1,112,128]{2,1,0:T(8,128)(2,1)S(1)}, bf16[1,112,128]{2,1,0:T(8,128)(2,1)S(1)}, u32[]{:S(2)}, u32[]{:S(2)}) collective-permute-start(bf16[1,112,128]{2,1,0:T(8,128)(2,1)S(1)} %shard_map.124.refs_7_.refs_0_), channel_id=1, source_target_pairs={{0,8},{1,9},{2,10},{3,11},{4,12},{5,13},{6,14},{7,15},{8,0},{9,1},... | collective-permute-start | bytes 86024 | tf_op jit(solution)/shard_map/ppermute | solution.py:272
  47.8 7.0 %collective-permute-start.20 = (bf16[4,112,128]{2,1,0:T(8,128)(2,1)S(1)}, bf16[4,112,128]{2,1,0:T(8,128)(2,1)S(1)}, u32[]{:S(2)}, u32[]{:S(2)}) collective-permute-start(bf16[4,112,128]{2,1,0:T(8,128)(2,1)S(1)} %shard_map.126.refs_0_), channel_id=1, source_target_pairs={{0,6},{1,7},{2,4},{3,5},{4,2},{5,3},{6,0},{7,1},{8,14},{9,15},{10,... | collective-permute-start | bytes 344072 | tf_op jit(solution)/shard_map/ppermute | solution.py:272
  49.2 6.9 %collective-permute-start.17 = (bf16[4,112,128]{2,1,0:T(8,128)(2,1)S(1)}, bf16[4,112,128]{2,1,0:T(8,128)(2,1)S(1)}, u32[]{:S(2)}, u32[]{:S(2)}) collective-permute-start(bf16[4,112,128]{2,1,0:T(8,128)(2,1)S(1)} %shard_map.126.refs_0_), channel_id=1, source_target_pairs={{0,4},{1,5},{2,6},{3,7},{4,0},{5,1},{6,2},{7,3},{8,12},{9,13},{10,... | collective-permute-start | bytes 344072 | tf_op jit(solution)/shard_map/ppermute | solution.py:272
  50.2 5.9 %collective-permute-start.16 = (bf16[4,112,128]{2,1,0:T(8,128)(2,1)S(1)}, bf16[4,112,128]{2,1,0:T(8,128)(2,1)S(1)}, u32[]{:S(2)}, u32[]{:S(2)}) collective-permute-start(bf16[4,112,128]{2,1,0:T(8,128)(2,1)S(1)} %shard_map.126.refs_0_), channel_id=1, source_target_pairs={{0,2},{1,3},{2,0},{3,1},{4,6},{5,7},{6,4},{7,5},{8,10},{9,11},{10,... | collective-permute-start | bytes 344072 | tf_op jit(solution)/shard_map/ppermute | solution.py:272
  51.4 5.2 %collective-permute-start.21 = (bf16[4,112,128]{2,1,0:T(8,128)(2,1)S(1)}, bf16[4,112,128]{2,1,0:T(8,128)(2,1)S(1)}, u32[]{:S(2)}, u32[]{:S(2)}) collective-permute-start(bf16[4,112,128]{2,1,0:T(8,128)(2,1)S(1)} %shard_map.126.refs_0_), channel_id=1, source_target_pairs={{0,1},{1,0},{2,3},{3,2},{4,5},{5,4},{6,7},{7,6},{8,9},{9,8},{10,11... | collective-permute-start | bytes 344072 | tf_op jit(solution)/shard_map/ppermute | solution.py:276
  54.8 1.8 %collective-permute-start.22 = (bf16[4,112,128]{2,1,0:T(8,128)(2,1)S(1)}, bf16[4,112,128]{2,1,0:T(8,128)(2,1)S(1)}, u32[]{:S(2)}, u32[]{:S(2)}) collective-permute-start(bf16[4,112,128]{2,1,0:T(8,128)(2,1)S(1)} %collective-permute-done.20.refs_1_), channel_id=1, source_target_pairs={{0,1},{1,0},{2,3},{3,2},{4,5},{5,4},{6,7},{7,6},{8,9},{9,8},{10,11... | collective-permute-start | bytes 344072 | tf_op jit(solution)/shard_map/ppermute | solution.py:276
  56.1 1.4 %collective-permute-start.19 = (bf16[4,112,128]{2,1,0:T(8,128)(2,1)S(1)}, bf16[4,112,128]{2,1,0:T(8,128)(2,1)S(1)}, u32[]{:S(2)}, u32[]{:S(2)}) collective-permute-start(bf16[4,112,128]{2,1,0:T(8,128)(2,1)S(1)} %collective-permute-done.17.refs_1_), channel_id=1, source_target_pairs={{0,1},{1,0},{2,3},{3,2},{4,5},{5,4},{6,7},{7,6},{8,9},{9,8},{10,11... | collective-permute-start | bytes 344072 | tf_op jit(solution)/shard_map/ppermute | solution.py:276
  56.1 1.5 %collective-permute-start.18 = (bf16[4,112,128]{2,1,0:T(8,128)(2,1)S(1)}, bf16[4,112,128]{2,1,0:T(8,128)(2,1)S(1)}, u32[]{:S(2)}, u32[]{:S(2)}) collective-permute-start(bf16[4,112,128]{2,1,0:T(8,128)(2,1)S(1)} %collective-permute-done.16.refs_0_), channel_id=1, source_target_pairs={{0,1},{1,0},{2,3},{3,2},{4,5},{5,4},{6,7},{7,6},{8,9},{9,8},{10,11... | collective-permute-start | bytes 344072 | tf_op jit(solution)/shard_map/ppermute | solution.py:276
